TPU v7x, 32 devices: a whole 2x2x4 slice. The times are simulated.
32 devices in a mesh: rep: 8 (over z, core), mdl: 4 (over y, x).
Axes of the slice: x: 2, y: 2, z: 4, core: 2. Of those that a mesh axis runs over, the one named last changes fastest.
Arguments:
- deltas: bfloat16 [8, 2560, 2560], P('rep', 'mdl'), may hold values from -72 to 72
- errors: bfloat16 [8, 2560, 2560], P('rep', 'mdl'), may hold values from -3 to 3
- starts: float32 [2560, 64], replicated, may hold values from -6 to 6
- momentum: float32 [2560, 2560], P('mdl', 'rep'), may hold values from -2 to 2
Outputs:
- new_errors: bfloat16 [8, 2560, 2560], P('rep', 'mdl')
- new_momentum: float32 [2560, 2560], P('mdl', 'rep')
- outer_step: float32 [2560, 2560], P('mdl', 'rep')
All inputs are finite; a program needn't handle non-finite values.
Results may differ from a plain program's by a relative error of at most 0.001.
Values sent between devices are 32-bit elements; how exact they have to be, the bound alone decides.
A program may use at most 64 MiB of HBM per device.

v0:
```python
import jax
import jax.numpy as jnp
from jax import lax
from jax.sharding import PartitionSpec as P

highest = lax.Precision.HIGHEST


def body(deltas, errors, starts, momentum):
    replicas = lax.axis_size("rep")
    merged = deltas[0].astype(jnp.float32) + errors[0].astype(jnp.float32)
    left_part = jnp.einsum("ac,ck->ka", merged, starts, precision=highest)
    left = lax.psum(left_part, "rep") / replicas
    gram = jnp.einsum("ka,la->kl", left, left, precision=highest)
    gram = lax.psum(gram, "mdl")
    lower = jnp.linalg.cholesky(gram)
    basis = jax.scipy.linalg.solve_triangular(lower, left, lower=True)
    right_part = jnp.einsum("ac,ka->kc", merged, basis, precision=highest)
    column_shares = lax.psum_scatter(right_part, "mdl", scatter_dimension=1, tiled=True)
    column_shares = lax.psum(column_shares, "rep")
    right = lax.all_gather(column_shares, "mdl", axis=1, tiled=True) / replicas
    approx = jnp.einsum("ka,kc->ac", basis, right, precision=highest)
    new_errors = (merged - approx).astype(jnp.bfloat16)[None]
    width = momentum.shape[1]
    owned = lax.dynamic_slice_in_dim(approx, lax.axis_index("rep") * width, width, 1)
    new_momentum = 0.9 * momentum + owned
    outer_step = 0.7 * (owned + 0.9 * new_momentum)
    return (new_errors, new_momentum, outer_step)


def solution(mesh):
    placed = (P("rep", "mdl", None), P("rep", "mdl", None), P(), P("mdl", "rep"))
    return jax.shard_map(
        body,
        mesh=mesh,
        in_specs=placed,
        out_specs=(P("rep", "mdl", None), P("mdl", "rep"), P("mdl", "rep")),
        check_vma=False,
    )
```

profile of v0, /device:TPU:0, one launch (start us, length us, event | category | flops | bytes accessed | tf_op | source)
XLA Modules:
  0.0 226.7 jit_solution(16170956885530419653)
XLA Ops:
  7.2 0.0 copy-start
  7.2 0.0 copy-start.3
  7.2 0.0 all-reduce.3.cloned.1.call-start
  7.2 1.0 copy-done
  8.3 9.4 %fusion.6 = f32[64,640]{1,0:T(8,128)} fusion(f32[2560,64]{0,1:T(8,128)S(1)} %copy-done, bf16[1,640,2560]{2,1,0:T(8,128)(2,1)} %param.5, bf16[1,640,2560]{2,1,0:T(8,128)(2,1)} %param.4), kind=kOutput, calls=%fused_computation.8 | convolution fusion | flops 1263206400 | bytes 7372800 | tf_op jit(solution)/shard_map/ac,ck->ka/dot_general | solution.py:12
  17.6 0.0 all-reduce.3.cloned.1.call-update
  17.7 0.0 reduce-scatter.2.cloned.1.call-start
  17.7 55.5 %all-reduce.3.cloned.1.call-done = f32[64,640]{1,0:T(8,128)} async-done(((f32[64,640]{1,0:T(8,128)}), f32[64,640]{1,0:T(8,128)}) %all-reduce.3.cloned.1.call-update) | async-done | bytes 163856 | tf_op jit(solution)/shard_map/psum | solution.py:13
  73.2 1.3 fusion.14
  74.5 16.2 %psum.22 = f32[64,64]{0,1:T(8,128)S(1)} all-reduce(f32[64,64]{0,1:T(8,128)S(1)} %fusion.14), channel_id=1, replica_groups=mesh['rep'=8,'mdl'=4] {'mdl'}, use_global_device_ids=true, to_apply=%region_1.0 | all-reduce | flops 4096 | bytes 32768 | tf_op jit(solution)/shard_map/psum | solution.py:15
  90.7 0.1 copy.8
  90.8 5.8 %cholesky.16 = f32[64,64]{1,0:T(8,128)S(1)} custom-call(f32[64,64]{1,0:T(8,128)S(1)} %fusion.20), custom_call_target="Cholesky" | custom-call | tf_op jit(solution)/shard_map/jit(cholesky)/cholesky | solution.py:16
  96.7 0.6 compare_reduce_fusion
  97.3 0.7 fusion.18
  98.0 4.9 %custom-call.7 = f32[1,64,64]{1,2,0:T(8,128)S(1)} custom-call(f32[1,64,64]{2,1,0:T(8,128)S(1)} %fusion.18), custom_call_target="InvertDiagBlocksLowerTriangular" | custom-call | tf_op jit(solution)/shard_map/jit(_solve_triangular)/triangular_solve | solution.py:17
  102.9 1.3 fusion.12
  104.2 8.3 %fusion = f32[64,2560]{1,0:T(8,128)} fusion(f32[64,640]{1,0:T(8,128)S(1)} %fusion.12, bf16[1,640,2560]{2,1,0:T(8,128)(2,1)} %param.5, bf16[1,640,2560]{2,1,0:T(8,128)(2,1)} %param.4), kind=kOutput, calls=%fused_computation.1 | convolution fusion | flops 1263206400 | bytes 7372800 | tf_op jit(solution)/shard_map/ac,ka->kc/dot_general | solution.py:18
  112.5 0.0 reduce-scatter.2.cloned.1.call-update
  112.5 0.0 all-reduce.5.cloned.1.call-start
  112.6 25.6 %reduce-scatter.2.cloned.1.call-done = f32[64,640]{1,0:T(8,128)} async-done(((f32[64,2560]{1,0:T(8,128)}), f32[64,640]{1,0:T(8,128)}) %reduce-scatter.2.cloned.1.call-update) | async-done | bytes 163856 | tf_op jit(solution)/shard_map/reduce_scatter | solution.py:19
  138.2 0.0 all-reduce.5.cloned.1.call-update
  138.3 0.0 copy-done.3
  138.3 0.3 copy.9
  138.6 54.7 %all-reduce.5.cloned.1.call-done = f32[64,640]{1,0:T(8,128)} async-done(((f32[64,640]{1,0:T(8,128)}), f32[64,640]{1,0:T(8,128)}) %all-reduce.5.cloned.1.call-update) | async-done | bytes 163856 | tf_op jit(solution)/shard_map/psum | solution.py:20
  193.3 13.2 %all_gather.3 = f32[64,2560]{1,0:T(8,128)S(1)} all-gather(f32[64,640]{1,0:T(8,128)} %all-reduce.5.cloned.1.call-done), channel_id=1, replica_groups=mesh['rep'=8,'mdl'=4] {'mdl'}, dimensions={1}, use_global_device_ids=true | all-gather | bytes 819200 | tf_op jit(solution)/shard_map/all_gather | solution.py:21
  206.4 5.4 %fusion.9 = f32[640,2560]{1,0:T(8,128)S(1)} fusion(f32[64,640]{1,0:T(8,128)S(1)} %fusion.12, f32[64,2560]{1,0:T(8,128)S(1)} %all_gather.3), kind=kOutput, calls=%fused_computation.11 | convolution fusion | flops 1258455040 | bytes 7372800 | tf_op jit(solution)/shard_map/ka,kc->ac/dot_general | solution.py:22
  211.9 0.0 copy-done.1
  211.9 0.0 copy-done.2
  211.9 3.3 %fusion.5 = bf16[1,640,2560]{2,1,0:T(8,128)(2,1)} fusion(f32[640,2560]{1,0:T(8,128)S(1)} %fusion.9, bf16[1,640,2560]{2,1,0:T(8,128)(2,1)S(1)} %copy-done.1, bf16[1,640,2560]{2,1,0:T(8,128)(2,1)S(1)} %copy-done.2), kind=kLoop, calls=%fused_computation.7 | loop fusion | flops 8192000 | bytes 16384000 | tf_op jit(solution)/shard_map/broadcast_in_dim | solution.py:23
  215.2 1.3 add_multiply_fusion
  216.5 2.4 %copy.10 = f32[640,320]{0,1:T(8,128)} copy(f32[640,320]{1,0:T(8,128)} %get-tuple-element.7) | data formatting | bytes 1638400
  218.9 1.2 copy.11
  (4 shorter events, 0.0 us)
Async XLA Ops:
  7.2 1.1 copy-start
  7.2 131.1 %copy-start.3 = (f32[640,320]{0,1:T(8,128)S(1)}, f32[640,320]{0,1:T(8,128)}, u32[]{:S(2)}) copy-start(f32[640,320]{0,1:T(8,128)} %param.7) | copy-start | bytes 2457604
  7.2 66.0 %all-reduce.3.cloned.1.call-start = ((), (), s32[]{:S(2)}) async-start(), calls=%async_computation.1 | async-start | bytes 327680 | tf_op jit(solution)/shard_map/psum | solution.py:13
  17.7 120.6 %reduce-scatter.2.cloned.1.call-start = ((), (), s32[]{:S(2)}) async-start(), calls=%async_computation.2 | async-start | bytes 819200 | tf_op jit(solution)/shard_map/reduce_scatter | solution.py:19
  112.5 80.7 %all-reduce.5.cloned.1.call-start = ((), (), s32[]{:S(2)}) async-start(), calls=%async_computation.3 | async-start | bytes 327680 | tf_op jit(solution)/shard_map/psum | solution.py:20
  193.3 18.6 %copy-start.1 = (bf16[1,640,2560]{2,1,0:T(8,128)(2,1)S(1)}, bf16[1,640,2560]{2,1,0:T(8,128)(2,1)}, u32[]{:S(2)}) copy-start(bf16[1,640,2560]{2,1,0:T(8,128)(2,1)} %param.5) | copy-start | bytes 9830404
  193.3 18.6 %copy-start.2 = (bf16[1,640,2560]{2,1,0:T(8,128)(2,1)S(1)}, bf16[1,640,2560]{2,1,0:T(8,128)(2,1)}, u32[]{:S(2)}) copy-start(bf16[1,640,2560]{2,1,0:T(8,128)(2,1)} %param.4) | copy-start | bytes 9830404
Sparse Core Ops, SparseCore 0:
  17.8 55.3 all-reduce.2
  112.7 25.5 reduce-scatter.1
  140.6 52.6 all-reduce.4
where the time goes:
time: 227 us
  waiting for transfers between devices  136 us (60%)
  blocking collectives  29.4 us (13%)
  matrix products  25.7 us (11%)
  other arithmetic  16.7 us (7%)
  between operations  13.8 us (6%)
  local copies, waits for them, and re-layouts  5.06 us (2%)
    psum x1, waiting for transfers between devices, body(): left = lax.psum(left_part, 'rep') / replicas  55.5 us
    psum x1, waiting for transfers between devices, body(): column_shares = lax.psum(column_shares, 'rep')  54.7 us
    reduce_scatter x1, waiting for transfers between devices, body(): lax.psum_scatter(right_part, 'mdl', scatter_dimension=1, tiled=True)  25.6 us
    psum x1, blocking collectives, body(): gram = lax.psum(gram, 'mdl')  16.2 us
    all_gather x1, blocking collectives, body(): right = lax.all_gather(column_shares, 'mdl', axis=1, tiled=True) / replicas  13.2 us
    dot_general x1, matrix products, body(): left_part = jnp.einsum('ac,ck->ka', merged, starts, precision=highest)  9.37 us
    dot_general x1, matrix products, body(): right_part = jnp.einsum('ac,ka->kc', merged, basis, precision=highest)  8.35 us
    another operation x3, other arithmetic, body(): lower = jnp.linalg.cholesky(gram)  6.52 us
  transfers between devices with their start and end apart: 3, of which 3 were waited for; matrix products, arithmetic and copies ran while one was open for 0% of the time, Pallas kernels for 0%

commit v1 on v0

--- a/solution.py
+++ b/solution.py
@@ -4,6 +4,14 @@
 from jax.sharding import PartitionSpec as P
 
 highest = lax.Precision.HIGHEST
+
+
+def doubling_sum(x, axis):
+    n_dev, acc = (lax.axis_size(axis), x)
+    for hop in [1 << k for k in range(n_dev.bit_length() - 1)]:
+        swap = [(i, i ^ hop) for i in range(n_dev)]
+        acc = acc + lax.ppermute(acc, axis, swap)
+    return acc
 
 
 def body(deltas, errors, starts, momentum):
@@ -17,7 +25,7 @@
     basis = jax.scipy.linalg.solve_triangular(lower, left, lower=True)
     right_part = jnp.einsum("ac,ka->kc", merged, basis, precision=highest)
     column_shares = lax.psum_scatter(right_part, "mdl", scatter_dimension=1, tiled=True)
-    column_shares = lax.psum(column_shares, "rep")
+    column_shares = doubling_sum(column_shares, "rep")
     right = lax.all_gather(column_shares, "mdl", axis=1, tiled=True) / replicas
     approx = jnp.einsum("ka,kc->ac", basis, right, precision=highest)
     new_errors = (merged - approx).astype(jnp.bfloat16)[None]

time: 227 us -> 190 us (0.84)
  waiting for transfers between devices: 136 us -> 94.6 us
  starting transfers between devices: 0.12 us -> 4.09 us
    psum x1 -> x0, waiting for transfers between devices: 54.7 us -> none  [body(): column_shares = lax.psum(column_shares, 'rep')]
    ppermute x0 -> x3, waiting for transfers between devices: none -> 13.4 us  [doubling_sum(): acc = acc + lax.ppermute(acc, axis, swap)]
    ppermute x0 -> x3, starting transfers between devices: none -> 4.01 us  [doubling_sum(): acc = acc + lax.ppermute(acc, axis, swap)]
  transfers between devices with their start and end apart: 3 -> 5, of which waited for: 3 -> 5; matrix products, arithmetic and copies ran while one was open for 0% -> 0% of each run, Pallas kernels for 0% -> 0%
where the time goes in v1:
time: 190 us; the launch traced here: 189 us
  waiting for transfers between devices  94.6 us (50%)
  blocking collectives  28.1 us (15%)
  matrix products  25.7 us (14%)
  other arithmetic  17.7 us (9%)
  between operations  14.1 us (7%)
  local copies, waits for them, and re-layouts  5.08 us (3%)
  starting transfers between devices  4.09 us (2%)
    psum x1, waiting for transfers between devices, body(): left = lax.psum(left_part, 'rep') / replicas  55.5 us
    reduce_scatter x1, waiting for transfers between devices, body(): lax.psum_scatter(right_part, 'mdl', scatter_dimension=1, tiled=True)  25.7 us
    psum x1, blocking collectives, body(): gram = lax.psum(gram, 'mdl')  16.2 us
    ppermute x3, waiting for transfers between devices, doubling_sum(): acc = acc + lax.ppermute(acc, axis, swap)  13.4 us
    all_gather x1, blocking collectives, body(): right = lax.all_gather(column_shares, 'mdl', axis=1, tiled=True) / replicas  11.9 us
    dot_general x1, matrix products, body(): left_part = jnp.einsum('ac,ck->ka', merged, starts, precision=highest)  9.38 us
    dot_general x1, matrix products, body(): right_part = jnp.einsum('ac,ka->kc', merged, basis, precision=highest)  8.35 us
    another operation x3, other arithmetic, body(): lower = jnp.linalg.cholesky(gram)  6.52 us
  transfers between devices with their start and end apart: 5, of which 5 were waited for; matrix products, arithmetic and copies ran while one was open for 0% of the time, Pallas kernels for 0%

profile of v1, /device:TPU:0, one launch (start us, length us, event | category | flops | bytes accessed | tf_op | source)
XLA Modules:
  0.0 189.4 jit_solution(16816747590317281007)
XLA Ops:
  7.2 0.0 copy-start
  7.2 0.0 all-reduce.2.cloned.1.call-start
  7.2 1.0 copy-done
  8.3 9.4 %fusion.6 = f32[64,640]{1,0:T(8,128)} fusion(f32[2560,64]{0,1:T(8,128)S(1)} %copy-done, bf16[1,640,2560]{2,1,0:T(8,128)(2,1)} %param.5, bf16[1,640,2560]{2,1,0:T(8,128)(2,1)} %param.4), kind=kOutput, calls=%fused_computation.8 | convolution fusion | flops 1263206400 | bytes 7372800 | tf_op jit(solution)/shard_map/ac,ck->ka/dot_general | solution.py:20
  17.6 0.0 all-reduce.2.cloned.1.call-update
  17.7 0.0 reduce-scatter.2.cloned.1.call-start
  17.7 55.5 %all-reduce.2.cloned.1.call-done = f32[64,640]{1,0:T(8,128)} async-done(((f32[64,640]{1,0:T(8,128)}), f32[64,640]{1,0:T(8,128)}) %all-reduce.2.cloned.1.call-update) | async-done | bytes 163856 | tf_op jit(solution)/shard_map/psum | solution.py:21
  73.2 1.3 fusion.14
  74.5 16.2 %psum.15 = f32[64,64]{0,1:T(8,128)S(1)} all-reduce(f32[64,64]{0,1:T(8,128)S(1)} %fusion.14), channel_id=1, replica_groups=mesh['rep'=8,'mdl'=4] {'mdl'}, use_global_device_ids=true, to_apply=%region_1.0 | all-reduce | flops 4096 | bytes 32768 | tf_op jit(solution)/shard_map/psum | solution.py:23
  90.7 0.1 copy.8
  90.8 5.8 %cholesky.16 = f32[64,64]{1,0:T(8,128)S(1)} custom-call(f32[64,64]{1,0:T(8,128)S(1)} %fusion.20), custom_call_target="Cholesky" | custom-call | tf_op jit(solution)/shard_map/jit(cholesky)/cholesky | solution.py:24
  96.7 0.6 compare_reduce_fusion
  97.3 0.7 fusion.18
  98.0 4.9 %custom-call.7 = f32[1,64,64]{1,2,0:T(8,128)S(1)} custom-call(f32[1,64,64]{2,1,0:T(8,128)S(1)} %fusion.18), custom_call_target="InvertDiagBlocksLowerTriangular" | custom-call | tf_op jit(solution)/shard_map/jit(_solve_triangular)/triangular_solve | solution.py:25
  102.9 1.3 fusion.12
  104.2 8.3 %fusion = f32[64,2560]{1,0:T(8,128)} fusion(f32[64,640]{1,0:T(8,128)S(1)} %fusion.12, bf16[1,640,2560]{2,1,0:T(8,128)(2,1)} %param.5, bf16[1,640,2560]{2,1,0:T(8,128)(2,1)} %param.4), kind=kOutput, calls=%fused_computation.1 | convolution fusion | flops 1263206400 | bytes 7372800 | tf_op jit(solution)/shard_map/ac,ka->kc/dot_general | solution.py:26
  112.5 0.0 reduce-scatter.2.cloned.1.call-update
  112.6 25.7 %reduce-scatter.2.cloned.1.call-done = f32[64,640]{1,0:T(8,128)} async-done(((f32[64,2560]{1,0:T(8,128)}), f32[64,640]{1,0:T(8,128)}) %reduce-scatter.2.cloned.1.call-update) | async-done | bytes 163856 | tf_op jit(solution)/shard_map/reduce_scatter | solution.py:27
  138.2 1.6 collective-permute-done
  139.8 0.9 add.45
  140.8 1.5 collective-permute-start.1
  142.3 4.8 %collective-permute-done.1 = f32[64,640]{1,0:T(8,128)S(1)} collective-permute-done((f32[64,640]{1,0:T(8,128)S(1)}, f32[64,640]{1,0:T(8,128)S(1)}, u32[]{:S(2)}, u32[]{:S(2)}) %collective-permute-start.1) | collective-permute-done | bytes 163872 | tf_op jit(solution)/shard_map/ppermute | solution.py:13
  147.1 2.5 %collective-permute-start.2 = (f32[64,640]{1,0:T(8,128)S(1)}, f32[64,640]{1,0:T(8,128)S(1)}, u32[]{:S(2)}, u32[]{:S(2)}) collective-permute-start(f32[64,640]{1,0:T(8,128)S(1)} %add.46), channel_id=1, source_target_pairs={{0,16},{4,20},{8,24},{12,28},{16,0},{20,4},{24,8},{28,12},{1,17},{... | collective-permute-start | bytes 491528 | tf_op jit(solution)/shard_map/ppermute | solution.py:13
  149.6 0.3 copy.9
  149.9 0.0 copy-start.1
  149.9 7.0 %collective-permute-done.2 = f32[64,640]{1,0:T(8,128)S(1)} collective-permute-done((f32[64,640]{1,0:T(8,128)S(1)}, f32[64,640]{1,0:T(8,128)S(1)}, u32[]{:S(2)}, u32[]{:S(2)}) %collective-permute-start.2) | collective-permute-done | bytes 163872 | tf_op jit(solution)/shard_map/ppermute | solution.py:13
  157.0 11.9 %all_gather.3 = f32[64,2560]{1,0:T(8,128)S(1)} all-gather(f32[64,640]{1,0:T(8,128)S(1)} %add.47), channel_id=1, replica_groups=mesh['rep'=8,'mdl'=4] {'mdl'}, dimensions={1}, use_global_device_ids=true | all-gather | bytes 819200 | tf_op jit(solution)/shard_map/all_gather | solution.py:29
  168.9 5.4 %fusion.9 = f32[640,2560]{1,0:T(8,128)S(1)} fusion(f32[64,640]{1,0:T(8,128)S(1)} %fusion.12, f32[64,2560]{1,0:T(8,128)S(1)} %all_gather.3), kind=kOutput, calls=%fused_computation.11 | convolution fusion | flops 1258455040 | bytes 7372800 | tf_op jit(solution)/shard_map/ka,kc->ac/dot_general | solution.py:30
  174.3 3.3 %fusion.5 = bf16[1,640,2560]{2,1,0:T(8,128)(2,1)} fusion(f32[640,2560]{1,0:T(8,128)S(1)} %fusion.9, bf16[1,640,2560]{2,1,0:T(8,128)(2,1)S(1)} %copy-done.1, bf16[1,640,2560]{2,1,0:T(8,128)(2,1)S(1)} %copy-done.2), kind=kLoop, calls=%fused_computation.7 | loop fusion | flops 8192000 | bytes 16384000 | tf_op jit(solution)/shard_map/broadcast_in_dim | solution.py:31
  177.7 1.3 add_multiply_fusion
  179.0 2.4 %copy.10 = f32[640,320]{0,1:T(8,128)} copy(f32[640,320]{1,0:T(8,128)} %get-tuple-element.7) | data formatting | bytes 1638400
  181.4 1.2 copy.11
  (10 shorter events, 0.1 us)
Async XLA Ops:
  7.2 1.1 copy-start
  7.2 66.0 %all-reduce.2.cloned.1.call-start = ((), (), s32[]{:S(2)}) async-start(), calls=%async_computation.1 | async-start | bytes 327680 | tf_op jit(solution)/shard_map/psum | solution.py:21
  17.6 131.9 %copy-start.3 = (f32[640,320]{0,1:T(8,128)S(1)}, f32[640,320]{0,1:T(8,128)}, u32[]{:S(2)}) copy-start(f32[640,320]{0,1:T(8,128)} %param.7) | copy-start | bytes 2457604
  17.7 120.6 %reduce-scatter.2.cloned.1.call-start = ((), (), s32[]{:S(2)}) async-start(), calls=%async_computation.2 | async-start | bytes 819200 | tf_op jit(solution)/shard_map/reduce_scatter | solution.py:27
  138.2 1.6 collective-permute-start
  140.8 6.3 %collective-permute-start.1 = (f32[64,640]{1,0:T(8,128)S(1)}, f32[64,640]{1,0:T(8,128)S(1)}, u32[]{:S(2)}, u32[]{:S(2)}) collective-permute-start(f32[64,640]{1,0:T(8,128)S(1)} %add.45), channel_id=1, source_target_pairs={{0,8},{4,12},{8,0},{12,4},{16,24},{20,28},{24,16},{28,20},{1,9},{5... | collective-permute-start | bytes 491528 | tf_op jit(solution)/shard_map/ppermute | solution.py:13
  147.1 9.9 %collective-permute-start.2 = (f32[64,640]{1,0:T(8,128)S(1)}, f32[64,640]{1,0:T(8,128)S(1)}, u32[]{:S(2)}, u32[]{:S(2)}) collective-permute-start(f32[64,640]{1,0:T(8,128)S(1)} %add.46), channel_id=1, source_target_pairs={{0,16},{4,20},{8,24},{12,28},{16,0},{20,4},{24,8},{28,12},{1,17},{... | collective-permute-start | bytes 491528 | tf_op jit(solution)/shard_map/ppermute | solution.py:13
  149.9 24.4 %copy-start.1 = (bf16[1,640,2560]{2,1,0:T(8,128)(2,1)S(1)}, bf16[1,640,2560]{2,1,0:T(8,128)(2,1)}, u32[]{:S(2)}) copy-start(bf16[1,640,2560]{2,1,0:T(8,128)(2,1)} %param.5) | copy-start | bytes 9830404
  149.9 24.4 %copy-start.2 = (bf16[1,640,2560]{2,1,0:T(8,128)(2,1)S(1)}, bf16[1,640,2560]{2,1,0:T(8,128)(2,1)}, u32[]{:S(2)}) copy-start(bf16[1,640,2560]{2,1,0:T(8,128)(2,1)} %param.4) | copy-start | bytes 9830404
Sparse Core Ops, SparseCore 0:
  17.8 55.3 all-reduce.1
  112.7 25.4 reduce-scatter.1
